TPU v7x, 512 devices: a whole 4x8x8 slice. The times are simulated.
512 devices in a mesh: leaf: 8 (over x, core), front: 64 (over y, z).
Axes of the slice: x: 4, y: 8, z: 8, core: 2. Of those that a mesh axis runs over, the one named last changes fastest.
Arguments:
- rhs_leaf: float32 [8, 32, 229376], P('leaf', None, 'front'), may hold values from -6 to 6
- rhs_sep: float32 [8, 32, 8192], P('leaf', None, 'front'), may hold values from -6 to 6
- leaf_inv: float32 [8, 1792, 128, 128], P('leaf', 'front')
- leaf_update: float32 [8, 1792, 128, 128], P('leaf', 'front'), may hold values from -0.09375 to 0.09375
- update_rows: int32 [8, 1792, 128], P('leaf', 'front'), may hold values from 0 to 128, as said below
- update_owner: int32 [8, 1792, 1], P('leaf', 'front'), may hold values from 0 to 63; in each aligned block of 28 rows (0 to 27, 28 to 55, ..., all dimensions but the last counted through in order) no two rows name the same one
- sep_inv: float32 [8, 64, 128, 128], P('leaf', 'front')
- sep_couple: float32 [8, 64, 128, 128], P('leaf', 'front'), may hold values from -0.375 to 0.375
Outputs:
- x_leaf: float32 [8, 32, 229376], P('leaf', None, 'front')
- x_sep: float32 [8, 32, 8192], P('leaf', None, 'front')
Inputs may be any that keep to these rules, and one draw needn't show every extreme that they name: `update_rows`: within each leaf front the entries below 128 are distinct; the entries equal to 128 mark padded rows and come last in the front; some front has 64 padded rows. `update_owner`: at most 1 of the 28 leaf fronts held by one index of front have the same owner, and some index of front reaches 1.
All inputs are finite; a program needn't handle non-finite values.
Results may differ from a plain program's by a relative error of at most 0.0001.
Values sent between devices are 32-bit elements; how exact they have to be, the bound alone decides.
No kernel may reach another device: no remote copies, remote signals or barrier semaphores. Data moves between devices by JAX's collectives and lax.ppermute only.
A program may use at most 64 MiB of HBM per device.

v0:
```python
import jax
import jax.numpy as jnp
from jax import lax
from jax.sharding import PartitionSpec as P


def from_behind(value, axis, steps):
    count = lax.axis_size(axis)
    initial, last = (max(0, -steps), min(count, count - steps))
    return lax.ppermute(value, axis, [(source, source + steps) for source in range(initial, last)])


def apply_blocks(matrices, vectors):
    return jnp.einsum("bik,rbk->rbi", matrices, vectors, precision=lax.Precision.HIGHEST)


def apply_transposed(matrices, vectors):
    return jnp.einsum("bki,rbk->rbi", matrices, vectors, precision=lax.Precision.HIGHEST)


def apply_map(matrix, vectors):
    return jnp.einsum("ik,rk->ri", matrix, vectors, precision=lax.Precision.HIGHEST)


def apply_map_transposed(matrix, vectors):
    return jnp.einsum("ki,rk->ri", matrix, vectors, precision=lax.Precision.HIGHEST)


def per_device(
    rhs_leaf, rhs_sep, leaf_inv, leaf_update, update_rows, update_owner, sep_inv, sep_couple
):
    block_rows = leaf_inv.shape[-1]
    front_count = leaf_inv.shape[1]
    rhs_count = rhs_leaf.shape[1]
    fronts = lax.axis_size("front")
    groups = lax.axis_size("leaf")
    right_leaf = rhs_leaf[0].reshape(rhs_count, front_count, block_rows)
    leaf_y = apply_blocks(leaf_inv[0], right_leaf)
    updates = apply_blocks(leaf_update[0], leaf_y)
    row_index = update_rows[0]
    owners = update_owner[0]
    live_mask = row_index < block_rows
    updates = jnp.where(live_mask[None], updates, 0.0)
    local_rows = jnp.minimum(row_index, block_rows - 1)
    targets = owners * block_rows + local_rows
    dense_term = jnp.zeros((rhs_count, fronts * block_rows), jnp.float32)
    dense_term = dense_term.at[:, targets.reshape(-1)].add(updates.reshape(rhs_count, -1))
    collected = lax.psum_scatter(dense_term, "front", scatter_dimension=1, tiled=True)
    reduced = rhs_sep[0] - collected
    inv_block = sep_inv[0, 0]
    couple = sep_couple[0, 0]

    def forward_turn(turn_index, current):
        before = from_behind(current, "leaf", 1)
        return apply_map(inv_block, reduced - apply_map(couple, before))

    solved = lax.fori_loop(0, groups - 1, forward_turn, apply_map(inv_block, reduced))

    def backward_turn(turn_index, current):
        coupled = apply_map_transposed(couple, current)
        after = from_behind(coupled, "leaf", -1)
        return apply_map_transposed(inv_block, solved - after)

    x_sep = lax.fori_loop(0, groups - 1, backward_turn, apply_map_transposed(inv_block, solved))
    gathered = lax.all_gather(x_sep, "front", axis=1, tiled=True)
    picked = jnp.take(gathered, targets.reshape(-1), axis=1).reshape(
        rhs_count, front_count, block_rows
    )
    picked = jnp.where(live_mask[None], picked, 0.0)
    residue = leaf_y - apply_transposed(leaf_update[0], picked)
    x_leaf = apply_transposed(leaf_inv[0], residue)
    return (x_leaf.reshape(1, rhs_count, front_count * block_rows), x_sep[None])


def solution(mesh):
    placed = (
        P("leaf", None, "front"),
        P("leaf", None, "front"),
        P("leaf", "front", None, None),
        P("leaf", "front", None, None),
        P("leaf", "front", None),
        P("leaf", "front", None),
        P("leaf", "front", None, None),
        P("leaf", "front", None, None),
    )
    return jax.shard_map(
        per_device,
        mesh=mesh,
        in_specs=placed,
        out_specs=(P("leaf", None, "front"), P("leaf", None, "front")),
        check_vma=False,
    )
```

profile of v0, /device:TPU:2, one launch (start us, length us, event | category | flops | bytes accessed | tf_op | source)
XLA Modules:
  0.0 480.7 jit_solution(9119982957623492532)
XLA Ops:
  7.2 1.2 reshape_squeeze.3
  8.5 0.7 broadcast_compare_fusion
  9.2 4.4 fusion.14
  13.7 3.0 fusion.28
  16.7 1.8 copy.17
  18.6 23.0 %scatter_custom_fusion = f32[32,8192]{0,1:T(8,128)} fusion(s32[3584]{0:T(1024)S(1)} %fusion.41, f32[3584,32]{1,0:T(8,128)} %copy.17, f32[]{:T(128)} %constant.20.clone.1), kind=kCustom, calls=%fused_computation.5 | custom fusion | flops 114688 | bytes 1049088 | tf_op jit(solution)/shard_map/scatter-add | solution.py:47
  41.7 0.6 copy-done.6
  42.4 251.3 %reduce-scatter.2.cloned.1.call-done = f32[32,128]{0,1:T(8,128)} async-done(((f32[32,8192]{0,1:T(8,128)}), f32[32,128]{0,1:T(8,128)}) %reduce-scatter.2.cloned.1.call-update) | async-done | bytes 16400 | tf_op jit(solution)/shard_map/reduce_scatter | solution.py:48
  293.7 0.8 bitcast_subtract_fusion
  294.6 0.2 fusion.44
  294.9 38.5 %while.20 = (s32[]{:T(128)}, f32[32,128]{1,0:T(8,128)S(1)}, f32[128,128]{1,0:T(8,128)S(1)}, f32[32,128]{1,0:T(8,128)S(1)}, f32[128,128]{1,0:T(8,128)S(1)}, /*index=5*/s32[]{:T(128)}) while((s32[]{:T(128)}, f32[32,128]{1,0:T(8,128)S(1)}, f32[128,128]{1,0:T(8,128)S(1)}, f32[32,128]{1,0:T(8,128)S(1)}, f32[128,128]{1,0:T(8,128)S(1)}, ...), condition=%wide.region_3.4_spmd, body=%wide.region_2.3_spmd.sunk | while | flops 12587010 | bytes 278637 | solution.py:57
  294.9 1.9 collective-permute-start
  296.8 3.1 collective-permute-done
  299.9 0.2 convolution_subtract_fusion.2
  300.1 0.2 fusion.76
  300.4 1.9 collective-permute-start
  302.3 3.1 collective-permute-done
  305.4 0.2 convolution_subtract_fusion.2
  305.6 0.2 fusion.76
  305.9 1.9 collective-permute-start
  307.8 3.1 collective-permute-done
  310.9 0.2 convolution_subtract_fusion.2
  311.1 0.2 fusion.76
  311.4 1.9 collective-permute-start
  313.3 3.1 collective-permute-done
  316.4 0.2 convolution_subtract_fusion.2
  316.6 0.2 fusion.76
  316.9 1.9 collective-permute-start
  318.8 3.1 collective-permute-done
  321.9 0.2 convolution_subtract_fusion.2
  322.1 0.2 fusion.76
  322.4 1.9 collective-permute-start
  324.3 3.1 collective-permute-done
  327.4 0.2 convolution_subtract_fusion.2
  327.6 0.2 fusion.76
  327.9 1.9 collective-permute-start
  329.8 3.1 collective-permute-done
  332.9 0.2 convolution_subtract_fusion.2
  333.1 0.2 fusion.76
  333.3 0.2 fusion.42
  333.5 36.1 %while.21 = (s32[]{:T(128)}, f32[32,128]{1,0:T(8,128)S(1)}, f32[128,128]{1,0:T(8,128)S(1)}, f32[32,128]{1,0:T(8,128)S(1)}, f32[128,128]{1,0:T(8,128)S(1)}, /*index=5*/s32[]{:T(128)}) while((s32[]{:T(128)}, f32[32,128]{1,0:T(8,128)S(1)}, f32[128,128]{1,0:T(8,128)S(1)}, f32[32,128]{1,0:T(8,128)S(1)}, f32[128,128]{1,0:T(8,128)S(1)}, ...), condition=%wide.region_5.6_spmd, body=%wide.region_4.5_spmd.sunk | while | flops 12587010 | bytes 278637 | solution.py:64
  333.5 0.2 fusion.81
  333.7 1.9 collective-permute-start.1
  335.6 1.4 collective-permute-done.1
  337.2 0.2 fusion.81
  337.4 3.6 collective-permute-start.1
  341.0 1.4 collective-permute-done.1
  342.8 3.6 collective-permute-start.1
  346.4 1.4 collective-permute-done.1
  348.2 3.6 collective-permute-start.1
  351.8 1.4 collective-permute-done.1
  353.6 3.6 collective-permute-start.1
  357.2 1.4 collective-permute-done.1
  359.0 3.6 collective-permute-start.1
  362.6 1.4 collective-permute-done.1
  364.4 3.6 collective-permute-start.1
  368.0 1.4 collective-permute-done.1
  369.6 0.7 copy.19
  370.5 85.2 %all-gather.2.cloned.1.call-done = f32[32,8192]{0,1:T(8,128)} async-done(((f32[32,128]{0,1:T(8,128)}), f32[32,8192]{0,1:T(8,128)}) %all-gather.2.cloned.1.call-update) | async-done | bytes 1048592 | tf_op jit(solution)/shard_map/all_gather | solution.py:65
  455.7 9.5 %gather_fusion = f32[3584,32]{1,0:T(8,128)} fusion(f32[32,8192]{0,1:T(8,128)} %all-gather.2.cloned.1.call-done, s32[4096]{0:T(1024)S(1)} %pad_clamp_fusion), kind=kCustom, calls=%fused_computation | custom fusion | bytes 931840 | tf_op jit(solution)/shard_map/jit(_take)/gather | solution.py:66
  465.2 5.8 %fusion.31 = f32[32,28,128]{2,0,1:T(8,128)S(1)} fusion(f32[32,28,128]{2,0,1:T(8,128)S(1)} %fusion.14, f32[1,28,128,128]{3,2,1,0:T(8,128)S(1)} %copy-done, f32[32,28,128]{0,2,1:T(8,128)} %bitcast.100, pred[28,128]{1,0:T(8,128)(4,1)S(1)} %compare_and_fusion, pred[28,128]{1,0:T(8,128)(4,1)S(1)} %bitcast.104), kind=kOutput, calls=%fused_computation.22 | convolution fusion | flops 176504832 | bytes 3218432 | tf_op jit(solution)/shard_map/bki,rbk->rbi/dot_general | solution.py:18
  471.0 1.7 fusion.17
  472.8 0.3 copy.20
  473.0 0.8 reshape.72
  (41 shorter events, 2.4 us)
Async XLA Ops:
  7.2 6.5 %copy-start = (f32[1,28,128,128]{3,2,1,0:T(8,128)S(1)}, f32[1,28,128,128]{3,2,1,0:T(8,128)}, u32[]{:S(2)}) copy-start(f32[1,28,128,128]{3,2,1,0:T(8,128)} %param.15) | copy-start | bytes 5505028
  7.2 286.5 %reduce-scatter.2.cloned.1.call-start = ((), (), s32[]{:S(2)}) async-start(), calls=%async_computation.1 | async-start | bytes 4259840 | tf_op jit(solution)/shard_map/reduce_scatter | solution.py:48
  16.6 1.9 copy-start.7
  16.6 1.9 copy-start.5
  41.6 0.7 copy-start.6
  41.6 253.0 %copy-start.1 = (f32[1,1,128,128]{3,2,1,0:T(8,128)S(1)}, f32[1,1,128,128]{3,2,1,0:T(8,128)}, u32[]{:S(2)}) copy-start(f32[1,1,128,128]{3,2,1,0:T(8,128)} %param.18) | copy-start | bytes 196612
  41.6 253.2 %copy-start.3 = (f32[1,1,128,128]{3,2,1,0:T(8,128)S(1)}, f32[1,1,128,128]{3,2,1,0:T(8,128)}, u32[]{:S(2)}) copy-start(f32[1,1,128,128]{3,2,1,0:T(8,128)} %param.19) | copy-start | bytes 196612
  41.6 414.1 %all-gather.2.cloned.1.call-start = ((), (), s32[]{:S(2)}) async-start(), calls=%async_computation.2 | async-start | bytes 4259840 | tf_op jit(solution)/shard_map/all_gather | solution.py:65
  294.9 5.1 %collective-permute-start = (f32[32,128]{1,0:T(8,128)S(1)}, f32[32,128]{1,0:T(8,128)S(1)}, u32[]{:S(2)}, u32[]{:S(2)}) collective-permute-start(f32[32,128]{1,0:T(8,128)S(1)} %get-tuple-element.157), channel_id=1, source_target_pairs={{0,64},{64,128},{128,192},{192,256},{256,320},{320,384},{384,448},... | collective-permute-start | bytes 49160 | tf_op jit(solution)/shard_map/while/body/eval_jaxpr/ppermute | solution.py:10
  300.4 5.1 %collective-permute-start = (f32[32,128]{1,0:T(8,128)S(1)}, f32[32,128]{1,0:T(8,128)S(1)}, u32[]{:S(2)}, u32[]{:S(2)}) collective-permute-start(f32[32,128]{1,0:T(8,128)S(1)} %get-tuple-element.157), channel_id=1, source_target_pairs={{0,64},{64,128},{128,192},{192,256},{256,320},{320,384},{384,448},... | collective-permute-start | bytes 49160 | tf_op jit(solution)/shard_map/while/body/eval_jaxpr/ppermute | solution.py:10
  305.9 5.1 %collective-permute-start = (f32[32,128]{1,0:T(8,128)S(1)}, f32[32,128]{1,0:T(8,128)S(1)}, u32[]{:S(2)}, u32[]{:S(2)}) collective-permute-start(f32[32,128]{1,0:T(8,128)S(1)} %get-tuple-element.157), channel_id=1, source_target_pairs={{0,64},{64,128},{128,192},{192,256},{256,320},{320,384},{384,448},... | collective-permute-start | bytes 49160 | tf_op jit(solution)/shard_map/while/body/eval_jaxpr/ppermute | solution.py:10
  311.4 5.1 %collective-permute-start = (f32[32,128]{1,0:T(8,128)S(1)}, f32[32,128]{1,0:T(8,128)S(1)}, u32[]{:S(2)}, u32[]{:S(2)}) collective-permute-start(f32[32,128]{1,0:T(8,128)S(1)} %get-tuple-element.157), channel_id=1, source_target_pairs={{0,64},{64,128},{128,192},{192,256},{256,320},{320,384},{384,448},... | collective-permute-start | bytes 49160 | tf_op jit(solution)/shard_map/while/body/eval_jaxpr/ppermute | solution.py:10
  316.9 5.1 %collective-permute-start = (f32[32,128]{1,0:T(8,128)S(1)}, f32[32,128]{1,0:T(8,128)S(1)}, u32[]{:S(2)}, u32[]{:S(2)}) collective-permute-start(f32[32,128]{1,0:T(8,128)S(1)} %get-tuple-element.157), channel_id=1, source_target_pairs={{0,64},{64,128},{128,192},{192,256},{256,320},{320,384},{384,448},... | collective-permute-start | bytes 49160 | tf_op jit(solution)/shard_map/while/body/eval_jaxpr/ppermute | solution.py:10
  322.4 5.1 %collective-permute-start = (f32[32,128]{1,0:T(8,128)S(1)}, f32[32,128]{1,0:T(8,128)S(1)}, u32[]{:S(2)}, u32[]{:S(2)}) collective-permute-start(f32[32,128]{1,0:T(8,128)S(1)} %get-tuple-element.157), channel_id=1, source_target_pairs={{0,64},{64,128},{128,192},{192,256},{256,320},{320,384},{384,448},... | collective-permute-start | bytes 49160 | tf_op jit(solution)/shard_map/while/body/eval_jaxpr/ppermute | solution.py:10
  327.9 5.1 %collective-permute-start = (f32[32,128]{1,0:T(8,128)S(1)}, f32[32,128]{1,0:T(8,128)S(1)}, u32[]{:S(2)}, u32[]{:S(2)}) collective-permute-start(f32[32,128]{1,0:T(8,128)S(1)} %get-tuple-element.157), channel_id=1, source_target_pairs={{0,64},{64,128},{128,192},{192,256},{256,320},{320,384},{384,448},... | collective-permute-start | bytes 49160 | tf_op jit(solution)/shard_map/while/body/eval_jaxpr/ppermute | solution.py:10
  333.7 3.4 collective-permute-start.1
  337.4 5.1 %collective-permute-start.1 = (f32[32,128]{1,0:T(8,128)S(1)}, f32[32,128]{1,0:T(8,128)S(1)}, u32[]{:S(2)}, u32[]{:S(2)}) collective-permute-start(f32[32,128]{1,0:T(8,128)S(1)} %fusion.81), channel_id=1, source_target_pairs={{64,0},{128,64},{192,128},{256,192},{320,256},{384,320},{448,384},... | collective-permute-start | bytes 49160 | tf_op jit(solution)/shard_map/while/body/eval_jaxpr/ppermute | solution.py:10
  342.8 5.1 %collective-permute-start.1 = (f32[32,128]{1,0:T(8,128)S(1)}, f32[32,128]{1,0:T(8,128)S(1)}, u32[]{:S(2)}, u32[]{:S(2)}) collective-permute-start(f32[32,128]{1,0:T(8,128)S(1)} %fusion.81), channel_id=1, source_target_pairs={{64,0},{128,64},{192,128},{256,192},{320,256},{384,320},{448,384},... | collective-permute-start | bytes 49160 | tf_op jit(solution)/shard_map/while/body/eval_jaxpr/ppermute | solution.py:10
  348.2 5.1 %collective-permute-start.1 = (f32[32,128]{1,0:T(8,128)S(1)}, f32[32,128]{1,0:T(8,128)S(1)}, u32[]{:S(2)}, u32[]{:S(2)}) collective-permute-start(f32[32,128]{1,0:T(8,128)S(1)} %fusion.81), channel_id=1, source_target_pairs={{64,0},{128,64},{192,128},{256,192},{320,256},{384,320},{448,384},... | collective-permute-start | bytes 49160 | tf_op jit(solution)/shard_map/while/body/eval_jaxpr/ppermute | solution.py:10
  353.6 5.1 %collective-permute-start.1 = (f32[32,128]{1,0:T(8,128)S(1)}, f32[32,128]{1,0:T(8,128)S(1)}, u32[]{:S(2)}, u32[]{:S(2)}) collective-permute-start(f32[32,128]{1,0:T(8,128)S(1)} %fusion.81), channel_id=1, source_target_pairs={{64,0},{128,64},{192,128},{256,192},{320,256},{384,320},{448,384},... | collective-permute-start | bytes 49160 | tf_op jit(solution)/shard_map/while/body/eval_jaxpr/ppermute | solution.py:10
  359.0 5.1 %collective-permute-start.1 = (f32[32,128]{1,0:T(8,128)S(1)}, f32[32,128]{1,0:T(8,128)S(1)}, u32[]{:S(2)}, u32[]{:S(2)}) collective-permute-start(f32[32,128]{1,0:T(8,128)S(1)} %fusion.81), channel_id=1, source_target_pairs={{64,0},{128,64},{192,128},{256,192},{320,256},{384,320},{448,384},... | collective-permute-start | bytes 49160 | tf_op jit(solution)/shard_map/while/body/eval_jaxpr/ppermute | solution.py:10
  364.4 5.1 %collective-permute-start.1 = (f32[32,128]{1,0:T(8,128)S(1)}, f32[32,128]{1,0:T(8,128)S(1)}, u32[]{:S(2)}, u32[]{:S(2)}) collective-permute-start(f32[32,128]{1,0:T(8,128)S(1)} %fusion.81), channel_id=1, source_target_pairs={{64,0},{128,64},{192,128},{256,192},{320,256},{384,320},{448,384},... | collective-permute-start | bytes 49160 | tf_op jit(solution)/shard_map/while/body/eval_jaxpr/ppermute | solution.py:10
  369.6 95.6 %copy-start.4 = (f32[32,128]{1,0:T(8,128)}, f32[32,128]{1,0:T(8,128)S(1)}, u32[]{:S(2)}) copy-start(f32[32,128]{1,0:T(8,128)S(1)} %get-tuple-element.57) | copy-start | bytes 49156
  465.2 5.8 %copy-start.2 = (f32[1,28,128,128]{3,2,1,0:T(8,128)S(1)}, f32[1,28,128,128]{3,2,1,0:T(8,128)}, u32[]{:S(2)}) copy-start(f32[1,28,128,128]{3,2,1,0:T(8,128)} %param.14) | copy-start | bytes 5505028
Sparse Core Ops, SparseCore 0:
  41.7 251.8 reduce-scatter.1
  370.5 85.1 all-gather.1
where the time goes:
time: 481 us
  waiting for transfers between devices  368 us (77%)
  starting transfers between devices  37.2 us (8%)
  other arithmetic  24.7 us (5%)
  matrix products  20.3 us (4%)
  local copies, waits for them, and re-layouts  15.4 us (3%)
  between operations  14.2 us (3%)
    reduce_scatter x1, waiting for transfers between devices, per_device(): lax.psum_scatter(dense_term, 'front', scatter_dimension=1, tiled=True)  251 us
    all_gather x1, waiting for transfers between devices, per_device(): gathered = lax.all_gather(x_sep, 'front', axis=1, tiled=True)  85.2 us
    ppermute x14, starting transfers between devices, from_behind(): lax.ppermute(value, axis, [(source, source + steps) for source in range(i...  37.2 us
    ppermute x14, waiting for transfers between devices, from_behind(): lax.ppermute(value, axis, [(source, source + steps) for source in range(i...  31.9 us
    scatter-add x1, other arithmetic, per_device(): dense_term.at[:, targets.reshape(-1)].add(updates.reshape(rhs_count, -1))  23 us
  transfers between devices with their start and end apart: 16, of which 16 were waited for; matrix products, arithmetic and copies ran while one was open for 0% of the time, Pallas kernels for 0%

commit v1 on v0

--- a/solution.py
+++ b/solution.py
@@ -62,7 +62,8 @@
         return apply_map_transposed(inv_block, solved - after)
 
     x_sep = lax.fori_loop(0, groups - 1, backward_turn, apply_map_transposed(inv_block, solved))
-    gathered = lax.all_gather(x_sep, "front", axis=1, tiled=True)
+    sent = jnp.stack([x_sep] * lax.axis_size("front"))
+    gathered = jnp.concatenate(lax.all_to_all(sent, "front", 0, 0), axis=1)
     picked = jnp.take(gathered, targets.reshape(-1), axis=1).reshape(
         rhs_count, front_count, block_rows
     )

time: 481 us -> 438 us (0.911)
  the two profiles are of different devices: /device:TPU:2 before, /device:TPU:21 now
where the time goes in v1:
time: 438 us; the launch traced here: 437 us
  waiting for transfers between devices  304 us (69%)
  starting transfers between devices  57.2 us (13%)
  other arithmetic  24.7 us (6%)
  local copies, waits for them, and re-layouts  20.5 us (5%)
  matrix products  16.2 us (4%)
  between operations  14.2 us (3%)
    reduce_scatter x1, waiting for transfers between devices, per_device(): lax.psum_scatter(dense_term, 'front', scatter_dimension=1, tiled=True)  246 us
    ppermute x14, starting transfers between devices, from_behind(): lax.ppermute(value, axis, [(source, source + steps) for source in range(i...  48.5 us
    all_to_all x1, waiting for transfers between devices, per_device(): gathered = jnp.concatenate(lax.all_to_all(sent, 'front', 0, 0), axis=1)  30.5 us
    ppermute x14, waiting for transfers between devices, from_behind(): lax.ppermute(value, axis, [(source, source + steps) for source in range(i...  26.9 us
    scatter-add x1, other arithmetic, per_device(): dense_term.at[:, targets.reshape(-1)].add(updates.reshape(rhs_count, -1))  22.9 us
    gather x2, local copies, waits for them, and re-layouts, per_device(): jnp.take(gathered, targets.reshape(-1), axis=1)  11.6 us
  transfers between devices with their start and end apart: 16, of which 16 were waited for; matrix products, arithmetic and copies ran while one was open for 0% of the time, Pallas kernels for 0%

profile of v1, /device:TPU:21, one launch (start us, length us, event | category | flops | bytes accessed | tf_op | source)
XLA Modules:
  0.0 436.8 jit_solution(10685243955041255400)
XLA Ops:
  7.2 1.2 reshape_squeeze.3
  8.5 0.7 broadcast_compare_fusion
  9.2 4.4 %fusion.12 = f32[32,28,128]{2,0,1:T(8,128)S(1)} fusion(f32[1,28,128,128]{3,2,1,0:T(8,128)} %param.14, f32[32,28,128]{2,1,0:T(8,128)S(1)} %reshape_squeeze.3), kind=kOutput, calls=%fused_computation.15 | convolution fusion | flops 176160768 | bytes 2752512 | tf_op jit(solution)/shard_map/bik,rbk->rbi/dot_general | solution.py:14
  13.7 3.0 fusion.27
  16.7 1.8 copy.24
  18.6 22.9 %scatter_custom_fusion = f32[32,8192]{0,1:T(8,128)} fusion(s32[3584]{0:T(1024)S(1)} %fusion.37, f32[3584,32]{1,0:T(8,128)} %copy.24, f32[]{:T(128)} %constant.20.clone.1), kind=kCustom, calls=%fused_computation.5 | custom fusion | flops 114688 | bytes 1049088 | tf_op jit(solution)/shard_map/scatter-add | solution.py:47
  41.6 0.7 copy-done.6
  42.4 246.1 %reduce-scatter.2.cloned.1.call-done = f32[32,128]{0,1:T(8,128)} async-done(((f32[32,8192]{0,1:T(8,128)}), f32[32,128]{0,1:T(8,128)}) %reduce-scatter.2.cloned.1.call-update) | async-done | bytes 16400 | tf_op jit(solution)/shard_map/reduce_scatter | solution.py:48
  288.5 0.8 bitcast_subtract_fusion
  289.4 0.2 fusion.40
  289.7 42.6 %while.20 = (s32[]{:T(128)}, f32[32,128]{1,0:T(8,128)S(1)}, f32[128,128]{1,0:T(8,128)S(1)}, f32[32,128]{1,0:T(8,128)S(1)}, f32[128,128]{1,0:T(8,128)S(1)}, /*index=5*/s32[]{:T(128)}) while((s32[]{:T(128)}, f32[32,128]{1,0:T(8,128)S(1)}, f32[128,128]{1,0:T(8,128)S(1)}, f32[32,128]{1,0:T(8,128)S(1)}, f32[128,128]{1,0:T(8,128)S(1)}, ...), condition=%wide.region_3.4_spmd, body=%wide.region_2.3_spmd.sunk | while | flops 12587010 | bytes 278637 | solution.py:57
  289.7 8.3 %collective-permute-start = (f32[32,128]{1,0:T(8,128)S(1)}, f32[32,128]{1,0:T(8,128)S(1)}, u32[]{:S(2)}, u32[]{:S(2)}) collective-permute-start(f32[32,128]{1,0:T(8,128)S(1)} %get-tuple-element.162), channel_id=1, source_target_pairs={{0,64},{64,128},{128,192},{192,256},{256,320},{320,384},{384,448},... | collective-permute-start | bytes 49160 | tf_op jit(solution)/shard_map/while/body/eval_jaxpr/ppermute | solution.py:10
  298.0 0.8 collective-permute-done
  298.8 0.2 convolution_subtract_fusion.2
  299.0 0.2 fusion.72
  299.3 4.2 collective-permute-start
  303.5 0.8 collective-permute-done
  304.3 0.2 convolution_subtract_fusion.2
  304.5 0.2 fusion.72
  304.8 4.2 collective-permute-start
  309.0 0.8 collective-permute-done
  309.8 0.2 convolution_subtract_fusion.2
  310.0 0.2 fusion.72
  310.3 4.2 collective-permute-start
  314.5 0.8 collective-permute-done
  315.3 0.2 convolution_subtract_fusion.2
  315.5 0.2 fusion.72
  315.8 4.2 collective-permute-start
  320.0 0.8 collective-permute-done
  320.8 0.2 convolution_subtract_fusion.2
  321.0 0.2 fusion.72
  321.2 4.2 collective-permute-start
  325.5 0.8 collective-permute-done
  326.3 0.2 convolution_subtract_fusion.2
  326.5 0.2 fusion.72
  326.7 4.2 collective-permute-start
  331.0 0.8 collective-permute-done
  331.8 0.2 convolution_subtract_fusion.2
  332.0 0.2 fusion.72
  332.4 38.3 %while.21 = (s32[]{:T(128)}, f32[32,128]{1,0:T(8,128)S(1)}, f32[128,128]{1,0:T(8,128)S(1)}, f32[32,128]{1,0:T(8,128)S(1)}, f32[128,128]{1,0:T(8,128)S(1)}, /*index=5*/s32[]{:T(128)}) while((s32[]{:T(128)}, f32[32,128]{1,0:T(8,128)S(1)}, f32[128,128]{1,0:T(8,128)S(1)}, f32[32,128]{1,0:T(8,128)S(1)}, f32[128,128]{1,0:T(8,128)S(1)}, ...), condition=%wide.region_5.6_spmd, body=%wide.region_4.5_spmd.sunk | while | flops 12587010 | bytes 278637 | solution.py:64
  332.6 3.4 collective-permute-start.1
  336.0 2.2 collective-permute-done.1
  338.6 1.9 collective-permute-start.1
  340.5 3.1 collective-permute-done.1
  344.0 1.9 collective-permute-start.1
  345.9 3.1 collective-permute-done.1
  349.4 1.9 collective-permute-start.1
  351.3 3.1 collective-permute-done.1
  354.8 1.9 collective-permute-start.1
  356.7 3.1 collective-permute-done.1
  360.1 1.9 collective-permute-start.1
  362.1 3.1 collective-permute-done.1
  365.5 1.9 collective-permute-start.1
  367.5 3.1 collective-permute-done.1
  370.8 1.1 stack.4
  371.9 8.7 %all-to-all-start = ((f32[64,32,128]{2,1,0:T(8,128)}), f32[64,32,128]{2,1,0:T(8,128)S(1)}, u32[]{:S(2)}, u32[]{:S(2)}) async-start(f32[64,32,128]{2,1,0:T(8,128)} %stack.4), calls=%async_computation.1 | async-start | bytes 2097152 | tf_op jit(solution)/shard_map/all_to_all | solution.py:66
  380.7 30.5 %all-to-all-done = f32[64,32,128]{2,1,0:T(8,128)S(1)} async-done(((f32[64,32,128]{2,1,0:T(8,128)}), f32[64,32,128]{2,1,0:T(8,128)S(1)}, u32[]{:S(2)}, u32[]{:S(2)}) %all-to-all-start) | async-done | bytes 1048608 | tf_op jit(solution)/shard_map/all_to_all | solution.py:66
  411.2 2.6 copy.26
  413.8 9.6 %gather_fusion = f32[3584,32]{1,0:T(8,128)} fusion(f32[32,8192]{0,1:T(8,128)} %bitcast.99, s32[4096]{0:T(1024)S(1)} %pad_clamp_fusion), kind=kCustom, calls=%fused_computation | custom fusion | bytes 931840 | tf_op jit(solution)/shard_map/jit(_take)/gather | solution.py:67
  423.4 2.0 copy.27
  425.4 1.7 fusion.21
  427.1 1.7 fusion.15
  428.8 0.3 copy.28
  429.1 0.8 reshape.82
  (42 shorter events, 2.9 us)
Async XLA Ops:
  7.2 6.5 %copy-start = (f32[1,28,128,128]{3,2,1,0:T(8,128)S(1)}, f32[1,28,128,128]{3,2,1,0:T(8,128)}, u32[]{:S(2)}) copy-start(f32[1,28,128,128]{3,2,1,0:T(8,128)} %param.15) | copy-start | bytes 5505028
  7.2 281.3 %reduce-scatter.2.cloned.1.call-start = ((), (), s32[]{:S(2)}) async-start(), calls=%async_computation.2 | async-start | bytes 4259840 | tf_op jit(solution)/shard_map/reduce_scatter | solution.py:48
  16.6 1.9 copy-start.7
  16.6 1.9 copy-start.5
  41.6 0.7 copy-start.6
  41.6 247.8 %copy-start.1 = (f32[1,1,128,128]{3,2,1,0:T(8,128)S(1)}, f32[1,1,128,128]{3,2,1,0:T(8,128)}, u32[]{:S(2)}) copy-start(f32[1,1,128,128]{3,2,1,0:T(8,128)} %param.18) | copy-start | bytes 196612
  41.6 248.1 %copy-start.3 = (f32[1,1,128,128]{3,2,1,0:T(8,128)S(1)}, f32[1,1,128,128]{3,2,1,0:T(8,128)}, u32[]{:S(2)}) copy-start(f32[1,1,128,128]{3,2,1,0:T(8,128)} %param.19) | copy-start | bytes 196612
  289.7 9.2 %collective-permute-start = (f32[32,128]{1,0:T(8,128)S(1)}, f32[32,128]{1,0:T(8,128)S(1)}, u32[]{:S(2)}, u32[]{:S(2)}) collective-permute-start(f32[32,128]{1,0:T(8,128)S(1)} %get-tuple-element.162), channel_id=1, source_target_pairs={{0,64},{64,128},{128,192},{192,256},{256,320},{320,384},{384,448},... | collective-permute-start | bytes 49160 | tf_op jit(solution)/shard_map/while/body/eval_jaxpr/ppermute | solution.py:10
  299.3 5.1 %collective-permute-start = (f32[32,128]{1,0:T(8,128)S(1)}, f32[32,128]{1,0:T(8,128)S(1)}, u32[]{:S(2)}, u32[]{:S(2)}) collective-permute-start(f32[32,128]{1,0:T(8,128)S(1)} %get-tuple-element.162), channel_id=1, source_target_pairs={{0,64},{64,128},{128,192},{192,256},{256,320},{320,384},{384,448},... | collective-permute-start | bytes 49160 | tf_op jit(solution)/shard_map/while/body/eval_jaxpr/ppermute | solution.py:10
  304.8 5.1 %collective-permute-start = (f32[32,128]{1,0:T(8,128)S(1)}, f32[32,128]{1,0:T(8,128)S(1)}, u32[]{:S(2)}, u32[]{:S(2)}) collective-permute-start(f32[32,128]{1,0:T(8,128)S(1)} %get-tuple-element.162), channel_id=1, source_target_pairs={{0,64},{64,128},{128,192},{192,256},{256,320},{320,384},{384,448},... | collective-permute-start | bytes 49160 | tf_op jit(solution)/shard_map/while/body/eval_jaxpr/ppermute | solution.py:10
  310.3 5.1 %collective-permute-start = (f32[32,128]{1,0:T(8,128)S(1)}, f32[32,128]{1,0:T(8,128)S(1)}, u32[]{:S(2)}, u32[]{:S(2)}) collective-permute-start(f32[32,128]{1,0:T(8,128)S(1)} %get-tuple-element.162), channel_id=1, source_target_pairs={{0,64},{64,128},{128,192},{192,256},{256,320},{320,384},{384,448},... | collective-permute-start | bytes 49160 | tf_op jit(solution)/shard_map/while/body/eval_jaxpr/ppermute | solution.py:10
  315.8 5.1 %collective-permute-start = (f32[32,128]{1,0:T(8,128)S(1)}, f32[32,128]{1,0:T(8,128)S(1)}, u32[]{:S(2)}, u32[]{:S(2)}) collective-permute-start(f32[32,128]{1,0:T(8,128)S(1)} %get-tuple-element.162), channel_id=1, source_target_pairs={{0,64},{64,128},{128,192},{192,256},{256,320},{320,384},{384,448},... | collective-permute-start | bytes 49160 | tf_op jit(solution)/shard_map/while/body/eval_jaxpr/ppermute | solution.py:10
  321.2 5.1 %collective-permute-start = (f32[32,128]{1,0:T(8,128)S(1)}, f32[32,128]{1,0:T(8,128)S(1)}, u32[]{:S(2)}, u32[]{:S(2)}) collective-permute-start(f32[32,128]{1,0:T(8,128)S(1)} %get-tuple-element.162), channel_id=1, source_target_pairs={{0,64},{64,128},{128,192},{192,256},{256,320},{320,384},{384,448},... | collective-permute-start | bytes 49160 | tf_op jit(solution)/shard_map/while/body/eval_jaxpr/ppermute | solution.py:10
  326.7 5.1 %collective-permute-start = (f32[32,128]{1,0:T(8,128)S(1)}, f32[32,128]{1,0:T(8,128)S(1)}, u32[]{:S(2)}, u32[]{:S(2)}) collective-permute-start(f32[32,128]{1,0:T(8,128)S(1)} %get-tuple-element.162), channel_id=1, source_target_pairs={{0,64},{64,128},{128,192},{192,256},{256,320},{320,384},{384,448},... | collective-permute-start | bytes 49160 | tf_op jit(solution)/shard_map/while/body/eval_jaxpr/ppermute | solution.py:10
  332.6 5.6 %collective-permute-start.1 = (f32[32,128]{1,0:T(8,128)S(1)}, f32[32,128]{1,0:T(8,128)S(1)}, u32[]{:S(2)}, u32[]{:S(2)}) collective-permute-start(f32[32,128]{1,0:T(8,128)S(1)} %fusion.77), channel_id=1, source_target_pairs={{64,0},{128,64},{192,128},{256,192},{320,256},{384,320},{448,384},... | collective-permute-start | bytes 49160 | tf_op jit(solution)/shard_map/while/body/eval_jaxpr/ppermute | solution.py:10
  338.6 5.1 %collective-permute-start.1 = (f32[32,128]{1,0:T(8,128)S(1)}, f32[32,128]{1,0:T(8,128)S(1)}, u32[]{:S(2)}, u32[]{:S(2)}) collective-permute-start(f32[32,128]{1,0:T(8,128)S(1)} %fusion.77), channel_id=1, source_target_pairs={{64,0},{128,64},{192,128},{256,192},{320,256},{384,320},{448,384},... | collective-permute-start | bytes 49160 | tf_op jit(solution)/shard_map/while/body/eval_jaxpr/ppermute | solution.py:10
  344.0 5.1 %collective-permute-start.1 = (f32[32,128]{1,0:T(8,128)S(1)}, f32[32,128]{1,0:T(8,128)S(1)}, u32[]{:S(2)}, u32[]{:S(2)}) collective-permute-start(f32[32,128]{1,0:T(8,128)S(1)} %fusion.77), channel_id=1, source_target_pairs={{64,0},{128,64},{192,128},{256,192},{320,256},{384,320},{448,384},... | collective-permute-start | bytes 49160 | tf_op jit(solution)/shard_map/while/body/eval_jaxpr/ppermute | solution.py:10
  349.4 5.1 %collective-permute-start.1 = (f32[32,128]{1,0:T(8,128)S(1)}, f32[32,128]{1,0:T(8,128)S(1)}, u32[]{:S(2)}, u32[]{:S(2)}) collective-permute-start(f32[32,128]{1,0:T(8,128)S(1)} %fusion.77), channel_id=1, source_target_pairs={{64,0},{128,64},{192,128},{256,192},{320,256},{384,320},{448,384},... | collective-permute-start | bytes 49160 | tf_op jit(solution)/shard_map/while/body/eval_jaxpr/ppermute | solution.py:10
  354.8 5.1 %collective-permute-start.1 = (f32[32,128]{1,0:T(8,128)S(1)}, f32[32,128]{1,0:T(8,128)S(1)}, u32[]{:S(2)}, u32[]{:S(2)}) collective-permute-start(f32[32,128]{1,0:T(8,128)S(1)} %fusion.77), channel_id=1, source_target_pairs={{64,0},{128,64},{192,128},{256,192},{320,256},{384,320},{448,384},... | collective-permute-start | bytes 49160 | tf_op jit(solution)/shard_map/while/body/eval_jaxpr/ppermute | solution.py:10
  360.1 5.1 %collective-permute-start.1 = (f32[32,128]{1,0:T(8,128)S(1)}, f32[32,128]{1,0:T(8,128)S(1)}, u32[]{:S(2)}, u32[]{:S(2)}) collective-permute-start(f32[32,128]{1,0:T(8,128)S(1)} %fusion.77), channel_id=1, source_target_pairs={{64,0},{128,64},{192,128},{256,192},{320,256},{384,320},{448,384},... | collective-permute-start | bytes 49160 | tf_op jit(solution)/shard_map/while/body/eval_jaxpr/ppermute | solution.py:10
  365.5 5.1 %collective-permute-start.1 = (f32[32,128]{1,0:T(8,128)S(1)}, f32[32,128]{1,0:T(8,128)S(1)}, u32[]{:S(2)}, u32[]{:S(2)}) collective-permute-start(f32[32,128]{1,0:T(8,128)S(1)} %fusion.77), channel_id=1, source_target_pairs={{64,0},{128,64},{192,128},{256,192},{320,256},{384,320},{448,384},... | collective-permute-start | bytes 49160 | tf_op jit(solution)/shard_map/while/body/eval_jaxpr/ppermute | solution.py:10
  370.8 43.0 %copy-start.4 = (f32[32,128]{1,0:T(8,128)}, f32[32,128]{1,0:T(8,128)S(1)}, u32[]{:S(2)}) copy-start(f32[32,128]{1,0:T(8,128)S(1)} %get-tuple-element.57) | copy-start | bytes 49156
  371.9 39.3 %all-to-all-start = ((f32[64,32,128]{2,1,0:T(8,128)}), f32[64,32,128]{2,1,0:T(8,128)S(1)}, u32[]{:S(2)}, u32[]{:S(2)}) async-start(f32[64,32,128]{2,1,0:T(8,128)} %stack.4), calls=%async_computation.1 | async-start | bytes 2097152 | tf_op jit(solution)/shard_map/all_to_all | solution.py:66
  425.4 1.7 copy-start.2
Sparse Core Ops, SparseCore 0:
  41.7 246.7 reduce-scatter.1
